TPU v7x, 32 devices: a whole 2x2x4 slice. The times are simulated.
32 devices in a mesh: pole: 2 (over y), row: 4 (over x, core), col: 4 (over z).
Axes of the slice: x: 2, y: 2, z: 4, core: 2. Of those that a mesh axis runs over, the one named last changes fastest.
Arguments:
- inverse_blocks: float32 [4096, 2048], P(('pole', 'row'), 'col'), parts along dimension 0, may hold values from -6 to 6
- lower_panel: float32 [4096, 512], P(('pole', 'row'), 'col'), parts along dimension 0, may hold values from -0.125 to 0.125
- struct_mask: int32 [16, 4], P('row', 'col'), may hold values 0 or 1
- diag_inverse: float32 [1024, 128], P(('pole', 'col')), parts along dimension 0, may hold values from -6 to 6
Outputs:
- g_panel: float32 [4096, 512], P(('pole', 'row'), 'col'), parts along dimension 0
- g_diag: float32 [1024, 128], P(('pole', 'col')), parts along dimension 0
There are 2 independent parts, one for each index of `pole`. A program takes and returns all parts, laid end to end along the dimension named above; an argument that names none is the same for every part. Nothing has to cross between parts.
All inputs are finite; a program needn't handle non-finite values. No bound on the sum of `struct_mask` on one device may be relied on, other than what follows from the above.
Results may differ from a plain program's by a relative error of at most 0.000071.
Values sent between devices are 32-bit elements; how exact they have to be, the bound alone decides.
No kernel may reach another device: no remote copies, remote signals or barrier semaphores. Data moves between devices by JAX's collectives and lax.ppermute only.
A program may use at most 64 MiB of HBM per device.

v0:
```python
import jax
import jax.numpy as jnp
from jax import lax
from jax.sharding import PartitionSpec as P


def from_root(x, axis, root):
    mine = lax.axis_index(axis) == root
    return lax.psum(jnp.where(mine, x, jnp.zeros_like(x)), axis)


def on_device(inverse_blocks, lower_panel, struct_mask, diag_inverse):
    width = diag_inverse.shape[1]
    local_rows = lower_panel.shape[0]
    local_cols = lower_panel.shape[1]
    supers = local_cols // width
    expanded = jnp.repeat(jnp.repeat(struct_mask, width, axis=0), width, axis=1).astype(jnp.float32)
    masked = lower_panel * expanded
    panel_row = lax.all_gather(masked, "col", axis=1, tiled=True)
    mirrored = from_root(panel_row, "row", lax.axis_index("col"))
    summed = lax.psum_scatter(
        lax.dot_general(
            mirrored,
            inverse_blocks,
            (((0,), (1,)), ((), ())),
            precision=lax.Precision.HIGHEST,
            preferred_element_type=jnp.float32,
        ),
        "col",
        scatter_dimension=0,
        tiled=True,
    )
    g_panel = -summed.T * expanded
    masked_three = masked.reshape(local_rows, supers, width)
    panel_three = g_panel.reshape(local_rows, supers, width)
    quad_part = -jnp.einsum(
        "jka,jkb->kab", masked_three, panel_three, precision=lax.Precision.HIGHEST
    )
    quad_total = lax.psum(quad_part, "row")
    g_diag = diag_inverse + quad_total.reshape(supers * width, width)
    return (g_panel, g_diag)


def solution(mesh):
    placed = (
        P(("pole", "row"), "col"),
        P(("pole", "row"), "col"),
        P("row", "col"),
        P(("pole", "col"), None),
    )
    return jax.shard_map(
        on_device,
        mesh=mesh,
        in_specs=placed,
        out_specs=(P(("pole", "row"), "col"), P(("pole", "col"), None)),
        check_vma=False,
    )
```

profile of v0, /device:TPU:0, one launch (start us, length us, event | category | flops | bytes accessed | tf_op | source)
XLA Modules:
  0.0 153.8 jit_solution(16746672606810595600)
XLA Ops:
  7.2 0.0 copy-start
  7.2 0.0 all-gather.2.cloned.1.call-start
  7.2 0.7 convert_bitcast_fusion
  8.0 0.1 broadcast_bitcast_fusion
  8.0 1.8 %broadcast_multiply_fusion = f32[512,128]{1,0:T(8,128)} fusion(f32[512,128]{1,0:T(8,128)} %param.5, f32[512]{0:T(512)S(1)} %broadcast_bitcast_fusion), kind=kLoop, calls=%fused_computation.5 | loop fusion | flops 65536 | bytes 526336 | tf_op jit(solution)/shard_map/mul | solution.py:18
  9.8 0.0 all-gather.2.cloned.1.call-update
  9.8 0.0 all-reduce.3.cloned.1.call-start
  9.9 33.2 %all-gather.2.cloned.1.call-done = f32[512,512]{1,0:T(8,128)} async-done(((f32[512,128]{1,0:T(8,128)}), f32[512,512]{1,0:T(8,128)}) %all-gather.2.cloned.1.call-update) | async-done | bytes 1048592 | tf_op jit(solution)/shard_map/all_gather | solution.py:19
  43.1 2.3 %broadcast_select_fusion = f32[512,512]{1,0:T(8,128)} fusion(f32[512,512]{1,0:T(8,128)} %all-gather.2.cloned.1.call-done, pred[]{:T(512)S(6)} %eq.3), kind=kLoop, calls=%fused_computation.1 | loop fusion | flops 262144 | bytes 2097153 | tf_op jit(solution)/shard_map/jit(_where)/select_n | solution.py:9
  45.4 0.0 all-reduce.3.cloned.1.call-update
  45.4 0.0 reduce-scatter.2.cloned.1.call-start
  45.5 34.4 %all-reduce.3.cloned.1.call-done = f32[512,512]{1,0:T(8,128)} async-done(((f32[512,512]{1,0:T(8,128)}), f32[512,512]{1,0:T(8,128)}) %all-reduce.3.cloned.1.call-update) | async-done | bytes 1048592 | tf_op jit(solution)/shard_map/psum | solution.py:9
  79.9 0.0 copy-done
  79.9 5.7 %fusion.2 = f32[512,512]{1,0:T(8,128)} fusion(f32[512,512]{1,0:T(8,128)} %all-reduce.3.cloned.1.call-done, f32[512,512]{1,0:T(8,128)S(1)} %copy-done), kind=kOutput, calls=%fused_computation.8 | convolution fusion | flops 1610612736 | bytes 3145728 | tf_op jit(solution)/shard_map/dot_general | solution.py:22
  85.6 0.0 reduce-scatter.2.cloned.1.call-update
  85.7 0.0 all-reduce.5.cloned.1.call-start
  85.7 27.6 %reduce-scatter.2.cloned.1.call-done = f32[128,512]{1,0:T(8,128)} async-done(((f32[512,512]{1,0:T(8,128)}), f32[128,512]{1,0:T(8,128)}) %reduce-scatter.2.cloned.1.call-update) | async-done | bytes 262160 | tf_op jit(solution)/shard_map/reduce_scatter | solution.py:21
  113.3 0.0 copy-done.1
  113.4 2.3 %convolution_negate_fusion = f32[128,128]{1,0:T(8,128)} fusion(f32[128,512]{1,0:T(8,128)} %reduce-scatter.2.cloned.1.call-done, f32[512]{0:T(512)S(1)} %broadcast_bitcast_fusion, f32[512,128]{1,0:T(8,128)S(1)} %copy-done.1), kind=kOutput, calls=%fused_computation | convolution fusion | flops 100876288 | bytes 591872 | tf_op jit(solution)/shard_map/jka,jkb->kab/dot_general | solution.py:36
  115.7 0.0 all-reduce.5.cloned.1.call-update
  115.8 0.0 copy-start.3
  115.8 0.8 copy.6
  116.6 29.2 %all-reduce.5.cloned.1.call-done = f32[128,128]{1,0:T(8,128)} async-done(((f32[128,128]{1,0:T(8,128)}), f32[128,128]{1,0:T(8,128)}) %all-reduce.5.cloned.1.call-update) | async-done | bytes 65552 | tf_op jit(solution)/shard_map/psum | solution.py:39
  145.8 1.5 add.9
  (5 shorter events, 0.0 us)
Async XLA Ops:
  7.2 72.7 %copy-start = (f32[512,512]{1,0:T(8,128)S(1)}, f32[512,512]{1,0:T(8,128)}, u32[]{:S(2)}) copy-start(f32[512,512]{1,0:T(8,128)} %param.4) | copy-start | bytes 3145732
  7.2 35.9 %all-gather.2.cloned.1.call-start = ((), (), s32[]{:S(2)}) async-start(), calls=%async_computation.1 | async-start | bytes 1310720 | tf_op jit(solution)/shard_map/all_gather | solution.py:19
  9.8 70.1 %all-reduce.3.cloned.1.call-start = ((), (), s32[]{:S(2)}) async-start(), calls=%async_computation.2 | async-start | bytes 2097152 | tf_op jit(solution)/shard_map/psum | solution.py:9
  45.4 67.9 %reduce-scatter.2.cloned.1.call-start = ((), (), s32[]{:S(2)}) async-start(), calls=%async_computation.3 | async-start | bytes 1310720 | tf_op jit(solution)/shard_map/reduce_scatter | solution.py:21
  85.6 27.7 %copy-start.1 = (f32[512,128]{1,0:T(8,128)S(1)}, f32[512,128]{1,0:T(8,128)}, u32[]{:S(2)}) copy-start(f32[512,128]{1,0:T(8,128)} %param.5) | copy-start | bytes 786436
  85.7 60.2 %all-reduce.5.cloned.1.call-start = ((), (), s32[]{:S(2)}) async-start(), calls=%async_computation.4 | async-start | bytes 131072 | tf_op jit(solution)/shard_map/psum | solution.py:39
  113.4 2.4 %copy-start.2 = (f32[128,512]{1,0:T(8,128)S(1)}, f32[128,512]{1,0:T(8,128)}, u32[]{:S(2)}) copy-start(f32[128,512]{1,0:T(8,128)} %reduce-scatter.2.cloned.1.call-done) | copy-start | bytes 786436
  115.8 30.1 %copy-start.3 = (f32[128,128]{1,0:T(8,128)S(1)}, f32[128,128]{1,0:T(8,128)}, u32[]{:S(2)}) copy-start(f32[128,128]{1,0:T(8,128)} %param.7) | copy-start | bytes 196612
Sparse Core Ops, SparseCore 0:
  10.1 32.8 all-gather.1
  45.6 34.2 all-reduce.2
  85.8 27.5 reduce-scatter.1
  116.1 29.6 all-reduce.4
where the time goes:
time: 154 us
  waiting for transfers between devices  124 us (81%)
  between operations  13.8 us (9%)
  matrix products  8.07 us (5%)
  other arithmetic  6.37 us (4%)
    psum x1, waiting for transfers between devices, from_root(): return lax.psum(jnp.where(mine, x, jnp.zeros_like(x)), axis)  34.4 us
    all_gather x1, waiting for transfers between devices, on_device(): panel_row = lax.all_gather(masked, 'col', axis=1, tiled=True)  33.2 us
    psum x1, waiting for transfers between devices, on_device(): quad_total = lax.psum(quad_part, 'row')  29.2 us
    reduce_scatter x1, waiting for transfers between devices, on_device(): lax.psum_scatter(lax.dot_general(mirrored, inverse_blocks, (((0,), (1,)),...  27.6 us
    dot_general x1, matrix products, on_device(): lax.dot_general(mirrored, inverse_blocks, (((0,), (1,)), ((), ())), preci...  5.73 us
  transfers between devices with their start and end apart: 4, of which 4 were waited for; matrix products, arithmetic and copies ran while one was open for 1% of the time, Pallas kernels for 0%

commit v1 on v0

--- a/solution.py
+++ b/solution.py
@@ -16,7 +16,12 @@
     supers = local_cols // width
     expanded = jnp.repeat(jnp.repeat(struct_mask, width, axis=0), width, axis=1).astype(jnp.float32)
     masked = lower_panel * expanded
-    panel_row = lax.all_gather(masked, "col", axis=1, tiled=True)
+    ring = [masked]
+    for hop in range(3):
+        ring.append(lax.ppermute(ring[-1], "col", [(dev, (dev + 1) % 4) for dev in range(4)]))
+    panel_row = jnp.roll(
+        jnp.concatenate(ring[::-1], axis=1), (lax.axis_index("col") + 1) * ring[0].shape[1], axis=1
+    )
     mirrored = from_root(panel_row, "row", lax.axis_index("col"))
     summed = lax.psum_scatter(
         lax.dot_general(

time: 154 us -> 148 us (0.961)
  waiting for transfers between devices: 124 us -> 116 us
  starting transfers between devices: 0.16 us -> 3.2 us
    all_gather x1 -> x0, waiting for transfers between devices: 33.2 us -> none  [on_device(): panel_row = lax.all_gather(masked, 'col', axis=1, tiled=True)]
    ppermute x0 -> x3, waiting for transfers between devices: none -> 26 us  [on_device(): lax.ppermute(ring[-1], 'col', [(dev, (dev + 1) % 4) for dev in range(4)])]
    ppermute x0 -> x3, starting transfers between devices: none -> 3.08 us  [on_device(): lax.ppermute(ring[-1], 'col', [(dev, (dev + 1) % 4) for dev in range(4)])]
  transfers between devices with their start and end apart: 4 -> 6, of which waited for: 4 -> 6; matrix products, arithmetic and copies ran while one was open for 1% -> 1% of each run, Pallas kernels for 0% -> 0%
where the time goes in v1:
time: 148 us
  waiting for transfers between devices  116 us (78%)
  between operations  13.8 us (9%)
  matrix products  8.01 us (5%)
  other arithmetic  5.73 us (4%)
  starting transfers between devices  3.2 us (2%)
    psum x1, waiting for transfers between devices, from_root(): return lax.psum(jnp.where(mine, x, jnp.zeros_like(x)), axis)  34 us
    psum x1, waiting for transfers between devices, on_device(): quad_total = lax.psum(quad_part, 'row')  28.5 us
    reduce_scatter x1, waiting for transfers between devices, on_device(): lax.psum_scatter(lax.dot_general(mirrored, inverse_blocks, (((0,), (1,)),...  27.6 us
    ppermute x3, waiting for transfers between devices, on_device(): lax.ppermute(ring[-1], 'col', [(dev, (dev + 1) % 4) for dev in range(4)])  26 us
    dot_general x1, matrix products, on_device(): lax.dot_general(mirrored, inverse_blocks, (((0,), (1,)), ((), ())), preci...  5.74 us
    ppermute x3, starting transfers between devices, on_device(): lax.ppermute(ring[-1], 'col', [(dev, (dev + 1) % 4) for dev in range(4)])  3.08 us
  transfers between devices with their start and end apart: 6, of which 6 were waited for; matrix products, arithmetic and copies ran while one was open for 1% of the time, Pallas kernels for 0%

profile of v1, /device:TPU:0, one launch (start us, length us, event | category | flops | bytes accessed | tf_op | source)
XLA Modules:
  0.0 148.1 jit_solution(10218133313188352761)
XLA Ops:
  7.2 0.0 all-reduce.3.cloned.1.call-start
  7.2 0.8 convert_bitcast_fusion
  8.0 0.1 broadcast_bitcast_fusion
  8.1 1.1 broadcast_multiply_fusion
  9.2 3.1 %collective-permute-start = (f32[512,128]{1,0:T(8,128)S(1)}, f32[512,128]{1,0:T(8,128)S(1)}, u32[]{:S(2)}, u32[]{:S(2)}) collective-permute-start(f32[512,128]{1,0:T(8,128)S(1)} %broadcast_multiply_fusion), channel_id=1, source_target_pairs={{0,1},{1,2},{2,3},{3,0},{4,5},{5,6},{6,7},{7,4},{8,9},{9,10},{10,1... | collective-permute-start | bytes 786440 | tf_op jit(solution)/shard_map/ppermute | solution.py:21
  12.2 8.3 %collective-permute-done = f32[512,128]{1,0:T(8,128)S(1)} collective-permute-done((f32[512,128]{1,0:T(8,128)S(1)}, f32[512,128]{1,0:T(8,128)S(1)}, u32[]{:S(2)}, u32[]{:S(2)}) %collective-permute-start) | collective-permute-done | bytes 262176 | tf_op jit(solution)/shard_map/ppermute | solution.py:21
  20.6 9.3 %collective-permute-done.1 = f32[512,128]{1,0:T(8,128)S(1)} collective-permute-done((f32[512,128]{1,0:T(8,128)S(1)}, f32[512,128]{1,0:T(8,128)S(1)}, u32[]{:S(2)}, u32[]{:S(2)}) %collective-permute-start.1) | collective-permute-done | bytes 262176 | tf_op jit(solution)/shard_map/ppermute | solution.py:21
  29.9 8.4 %collective-permute-done.2 = f32[512,128]{1,0:T(8,128)S(1)} collective-permute-done((f32[512,128]{1,0:T(8,128)S(1)}, f32[512,128]{1,0:T(8,128)S(1)}, u32[]{:S(2)}, u32[]{:S(2)}) %collective-permute-start.2) | collective-permute-done | bytes 262176 | tf_op jit(solution)/shard_map/ppermute | solution.py:21
  38.3 0.1 constant_dynamic-update-slice_fusion.4
  38.6 0.1 constant_dynamic-update-slice_fusion
  38.7 1.2 dynamic-slice_select_fusion
  39.9 0.0 all-reduce.3.cloned.1.call-update
  39.9 0.0 reduce-scatter.2.cloned.1.call-start
  40.0 34.0 %all-reduce.3.cloned.1.call-done = f32[512,512]{1,0:T(8,128)} async-done(((f32[512,512]{1,0:T(8,128)}), f32[512,512]{1,0:T(8,128)}) %all-reduce.3.cloned.1.call-update) | async-done | bytes 1048592 | tf_op jit(solution)/shard_map/psum | solution.py:9
  74.0 5.7 %fusion.2 = f32[512,512]{1,0:T(8,128)} fusion(f32[512,512]{1,0:T(8,128)} %all-reduce.3.cloned.1.call-done, f32[512,512]{1,0:T(8,128)S(1)} %copy-done), kind=kOutput, calls=%fused_computation.16 | convolution fusion | flops 1610612736 | bytes 3145728 | tf_op jit(solution)/shard_map/dot_general | solution.py:27
  79.7 0.0 reduce-scatter.2.cloned.1.call-update
  79.7 0.0 all-reduce.5.cloned.1.call-start
  79.8 27.6 %reduce-scatter.2.cloned.1.call-done = f32[128,512]{1,0:T(8,128)} async-done(((f32[512,512]{1,0:T(8,128)}), f32[128,512]{1,0:T(8,128)}) %reduce-scatter.2.cloned.1.call-update) | async-done | bytes 262160 | tf_op jit(solution)/shard_map/reduce_scatter | solution.py:26
  107.4 2.3 %convolution_negate_fusion = f32[128,128]{1,0:T(8,128)} fusion(f32[128,512]{1,0:T(8,128)} %reduce-scatter.2.cloned.1.call-done, f32[512]{0:T(512)S(1)} %broadcast_bitcast_fusion, f32[512,128]{1,0:T(8,128)S(1)} %copy-done.1), kind=kOutput, calls=%fused_computation | convolution fusion | flops 100876288 | bytes 591872 | tf_op jit(solution)/shard_map/jka,jkb->kab/dot_general | solution.py:41
  109.7 0.0 all-reduce.5.cloned.1.call-update
  109.7 1.0 fusion
  110.7 0.8 copy.6
  111.5 28.5 %all-reduce.5.cloned.1.call-done = f32[128,128]{1,0:T(8,128)} async-done(((f32[128,128]{1,0:T(8,128)}), f32[128,128]{1,0:T(8,128)}) %all-reduce.5.cloned.1.call-update) | async-done | bytes 65552 | tf_op jit(solution)/shard_map/psum | solution.py:44
  140.0 1.5 add.25
  (14 shorter events, 0.2 us)
Async XLA Ops:
  7.2 66.8 %copy-start = (f32[512,512]{1,0:T(8,128)S(1)}, f32[512,512]{1,0:T(8,128)}, u32[]{:S(2)}) copy-start(f32[512,512]{1,0:T(8,128)} %param.4) | copy-start | bytes 3145732
  7.2 31.2 %copy-start.1 = (f32[512,128]{1,0:T(8,128)S(1)}, f32[512,128]{1,0:T(8,128)}, u32[]{:S(2)}) copy-start(f32[512,128]{1,0:T(8,128)} %param.5) | copy-start | bytes 786436
  7.2 66.8 %all-reduce.3.cloned.1.call-start = ((), (), s32[]{:S(2)}) async-start(), calls=%async_computation.1 | async-start | bytes 2097152 | tf_op jit(solution)/shard_map/psum | solution.py:9
  9.2 11.4 %collective-permute-start = (f32[512,128]{1,0:T(8,128)S(1)}, f32[512,128]{1,0:T(8,128)S(1)}, u32[]{:S(2)}, u32[]{:S(2)}) collective-permute-start(f32[512,128]{1,0:T(8,128)S(1)} %broadcast_multiply_fusion), channel_id=1, source_target_pairs={{0,1},{1,2},{2,3},{3,0},{4,5},{5,6},{6,7},{7,4},{8,9},{9,10},{10,1... | collective-permute-start | bytes 786440 | tf_op jit(solution)/shard_map/ppermute | solution.py:21
  20.6 9.3 %collective-permute-start.1 = (f32[512,128]{1,0:T(8,128)S(1)}, f32[512,128]{1,0:T(8,128)S(1)}, u32[]{:S(2)}, u32[]{:S(2)}) collective-permute-start(f32[512,128]{1,0:T(8,128)S(1)} %collective-permute-done), channel_id=1, source_target_pairs={{0,1},{1,2},{2,3},{3,0},{4,5},{5,6},{6,7},{7,4},{8,9},{9,10},{10,1... | collective-permute-start | bytes 786440 | tf_op jit(solution)/shard_map/ppermute | solution.py:21
  29.9 8.4 %collective-permute-start.2 = (f32[512,128]{1,0:T(8,128)S(1)}, f32[512,128]{1,0:T(8,128)S(1)}, u32[]{:S(2)}, u32[]{:S(2)}) collective-permute-start(f32[512,128]{1,0:T(8,128)S(1)} %collective-permute-done.1), channel_id=1, source_target_pairs={{0,1},{1,2},{2,3},{3,0},{4,5},{5,6},{6,7},{7,4},{8,9},{9,10},{10,1... | collective-permute-start | bytes 786440 | tf_op jit(solution)/shard_map/ppermute | solution.py:21
  39.9 67.5 %reduce-scatter.2.cloned.1.call-start = ((), (), s32[]{:S(2)}) async-start(), calls=%async_computation.2 | async-start | bytes 1310720 | tf_op jit(solution)/shard_map/reduce_scatter | solution.py:26
  79.7 60.3 %copy-start.2 = (f32[128,128]{1,0:T(8,128)S(1)}, f32[128,128]{1,0:T(8,128)}, u32[]{:S(2)}) copy-start(f32[128,128]{1,0:T(8,128)} %param.7) | copy-start | bytes 196612
  79.7 60.3 %all-reduce.5.cloned.1.call-start = ((), (), s32[]{:S(2)}) async-start(), calls=%async_computation.3 | async-start | bytes 131072 | tf_op jit(solution)/shard_map/psum | solution.py:44
Sparse Core Ops, SparseCore 0:
  40.0 33.8 all-reduce.2
  79.8 27.5 reduce-scatter.1
  110.3 29.6 all-reduce.4

commit v2 on v0

--- a/solution.py
+++ b/solution.py
@@ -36,7 +36,11 @@
     quad_part = -jnp.einsum(
         "jka,jkb->kab", masked_three, panel_three, precision=lax.Precision.HIGHEST
     )
-    quad_total = lax.psum(quad_part, "row")
+    quad_total = quad_part
+    for hop in (1, 2):
+        quad_total = quad_total + lax.ppermute(
+            quad_total, "row", [(dev, dev ^ hop) for dev in range(4)]
+        )
     g_diag = diag_inverse + quad_total.reshape(supers * width, width)
     return (g_panel, g_diag)
 

time: 154 us -> 128 us (0.83)
  waiting for transfers between devices: 124 us -> 98.5 us
  starting transfers between devices: 0.16 us -> 1.73 us
    psum x1 -> x0, waiting for transfers between devices: 29.2 us -> none  [on_device(): quad_total = lax.psum(quad_part, 'row')]
    ppermute x0 -> x2, waiting for transfers between devices: none -> 3.16 us  [on_device(): lax.ppermute(quad_total, 'row', [(dev, dev ^ hop) for dev in range(4)])]
    ppermute x0 -> x2, starting transfers between devices: none -> 1.61 us  [on_device(): lax.ppermute(quad_total, 'row', [(dev, dev ^ hop) for dev in range(4)])]
  transfers between devices with their start and end apart: 4 -> 5, of which waited for: 4 -> 5; matrix products, arithmetic and copies ran while one was open for 1% -> 1% of each run, Pallas kernels for 0% -> 0%
where the time goes in v2:
time: 128 us
  waiting for transfers between devices  98.5 us (77%)
  between operations  13.8 us (11%)
  matrix products  7.43 us (6%)
  other arithmetic  5.53 us (4%)
  starting transfers between devices  1.73 us (1%)
    psum x1, waiting for transfers between devices, from_root(): return lax.psum(jnp.where(mine, x, jnp.zeros_like(x)), axis)  34.4 us
    all_gather x1, waiting for transfers between devices, on_device(): panel_row = lax.all_gather(masked, 'col', axis=1, tiled=True)  33.2 us
    reduce_scatter x1, waiting for transfers between devices, on_device(): lax.psum_scatter(lax.dot_general(mirrored, inverse_blocks, (((0,), (1,)),...  27.7 us
    dot_general x1, matrix products, on_device(): lax.dot_general(mirrored, inverse_blocks, (((0,), (1,)), ((), ())), preci...  5.72 us
    ppermute x2, waiting for transfers between devices, on_device(): lax.ppermute(quad_total, 'row', [(dev, dev ^ hop) for dev in range(4)])  3.16 us
  transfers between devices with their start and end apart: 5, of which 5 were waited for; matrix products, arithmetic and copies ran while one was open for 1% of the time, Pallas kernels for 0%

profile of v2, /device:TPU:0, one launch (start us, length us, event | category | flops | bytes accessed | tf_op | source)
XLA Modules:
  0.0 127.9 jit_solution(2569486048996821685)
XLA Ops:
  7.2 0.0 copy-start
  7.2 0.0 all-gather.2.cloned.1.call-start
  7.2 0.7 convert_bitcast_fusion
  8.0 0.1 broadcast_bitcast_fusion
  8.0 1.8 %broadcast_multiply_fusion = f32[512,128]{1,0:T(8,128)} fusion(f32[512,128]{1,0:T(8,128)} %param.5, f32[512]{0:T(512)S(1)} %broadcast_bitcast_fusion), kind=kLoop, calls=%fused_computation.6 | loop fusion | flops 65536 | bytes 526336 | tf_op jit(solution)/shard_map/mul | solution.py:18
  9.8 0.0 all-gather.2.cloned.1.call-update
  9.8 0.0 all-reduce.2.cloned.1.call-start
  9.9 33.2 %all-gather.2.cloned.1.call-done = f32[512,512]{1,0:T(8,128)} async-done(((f32[512,128]{1,0:T(8,128)}), f32[512,512]{1,0:T(8,128)}) %all-gather.2.cloned.1.call-update) | async-done | bytes 1048592 | tf_op jit(solution)/shard_map/all_gather | solution.py:19
  43.1 2.3 %broadcast_select_fusion = f32[512,512]{1,0:T(8,128)} fusion(f32[512,512]{1,0:T(8,128)} %all-gather.2.cloned.1.call-done, pred[]{:T(512)S(6)} %eq.3), kind=kLoop, calls=%fused_computation.2 | loop fusion | flops 262144 | bytes 2097153 | tf_op jit(solution)/shard_map/jit(_where)/select_n | solution.py:9
  45.4 0.0 all-reduce.2.cloned.1.call-update
  45.4 0.0 reduce-scatter.2.cloned.1.call-start
  45.5 34.4 %all-reduce.2.cloned.1.call-done = f32[512,512]{1,0:T(8,128)} async-done(((f32[512,512]{1,0:T(8,128)}), f32[512,512]{1,0:T(8,128)}) %all-reduce.2.cloned.1.call-update) | async-done | bytes 1048592 | tf_op jit(solution)/shard_map/psum | solution.py:9
  79.9 5.7 %fusion.3 = f32[512,512]{1,0:T(8,128)} fusion(f32[512,512]{1,0:T(8,128)} %all-reduce.2.cloned.1.call-done, f32[512,512]{1,0:T(8,128)S(1)} %copy-done), kind=kOutput, calls=%fused_computation.10 | convolution fusion | flops 1610612736 | bytes 3145728 | tf_op jit(solution)/shard_map/dot_general | solution.py:22
  85.6 0.0 reduce-scatter.2.cloned.1.call-update
  85.6 27.7 %reduce-scatter.2.cloned.1.call-done = f32[128,512]{1,0:T(8,128)} async-done(((f32[512,512]{1,0:T(8,128)}), f32[128,512]{1,0:T(8,128)}) %reduce-scatter.2.cloned.1.call-update) | async-done | bytes 262160 | tf_op jit(solution)/shard_map/reduce_scatter | solution.py:21
  113.3 1.7 %fusion = f32[1,128,128]{2,1,0:T(8,128)S(1)} fusion(f32[128,512]{1,0:T(8,128)} %reduce-scatter.2.cloned.1.call-done, f32[512]{0:T(512)S(1)} %broadcast_bitcast_fusion, f32[512,128]{1,0:T(8,128)S(1)} %copy-done.1), kind=kOutput, calls=%fused_computation.1 | convolution fusion | flops 100876288 | bytes 591872 | tf_op jit(solution)/shard_map/jka,jkb->kab/dot_general | solution.py:36
  115.0 0.1 collective-permute-start
  115.1 1.2 collective-permute-done
  116.4 1.5 %collective-permute-start.1 = (f32[1,128,128]{2,1,0:T(8,128)S(1)}, f32[1,128,128]{2,1,0:T(8,128)S(1)}, u32[]{:S(2)}, u32[]{:S(2)}) collective-permute-start(f32[1,128,128]{2,1,0:T(8,128)S(1)} %add.13), channel_id=1, source_target_pairs={{0,8},{4,12},{8,0},{12,4},{1,9},{5,13},{9,1},{13,5},{2,10},{6,14},... | collective-permute-start | bytes 196616 | tf_op jit(solution)/shard_map/ppermute | solution.py:41
  117.9 0.0 copy-done.2
  117.9 0.0 copy-start.3
  117.9 0.8 copy.6
  118.8 1.9 %collective-permute-done.1 = f32[1,128,128]{2,1,0:T(8,128)S(1)} collective-permute-done((f32[1,128,128]{2,1,0:T(8,128)S(1)}, f32[1,128,128]{2,1,0:T(8,128)S(1)}, u32[]{:S(2)}, u32[]{:S(2)}) %collective-permute-start.1) | collective-permute-done | bytes 65568 | tf_op jit(solution)/shard_map/ppermute | solution.py:41
  120.7 0.6 bitcast_add_fusion
  (7 shorter events, 0.0 us)
Async XLA Ops:
  7.2 72.7 %copy-start = (f32[512,512]{1,0:T(8,128)S(1)}, f32[512,512]{1,0:T(8,128)}, u32[]{:S(2)}) copy-start(f32[512,512]{1,0:T(8,128)} %param.4) | copy-start | bytes 3145732
  7.2 35.9 %all-gather.2.cloned.1.call-start = ((), (), s32[]{:S(2)}) async-start(), calls=%async_computation.1 | async-start | bytes 1310720 | tf_op jit(solution)/shard_map/all_gather | solution.py:19
  9.8 70.0 %all-reduce.2.cloned.1.call-start = ((), (), s32[]{:S(2)}) async-start(), calls=%async_computation.2 | async-start | bytes 2097152 | tf_op jit(solution)/shard_map/psum | solution.py:9
  45.4 67.9 %reduce-scatter.2.cloned.1.call-start = ((), (), s32[]{:S(2)}) async-start(), calls=%async_computation.3 | async-start | bytes 1310720 | tf_op jit(solution)/shard_map/reduce_scatter | solution.py:21
  85.6 27.7 %copy-start.1 = (f32[512,128]{1,0:T(8,128)S(1)}, f32[512,128]{1,0:T(8,128)}, u32[]{:S(2)}) copy-start(f32[512,128]{1,0:T(8,128)} %param.5) | copy-start | bytes 786436
  113.3 4.6 %copy-start.2 = (f32[128,512]{1,0:T(8,128)S(1)}, f32[128,512]{1,0:T(8,128)}, u32[]{:S(2)}) copy-start(f32[128,512]{1,0:T(8,128)} %reduce-scatter.2.cloned.1.call-done) | copy-start | bytes 786436
  115.0 1.3 %collective-permute-start = (f32[1,128,128]{2,1,0:T(8,128)S(1)}, f32[1,128,128]{2,1,0:T(8,128)S(1)}, u32[]{:S(2)}, u32[]{:S(2)}) collective-permute-start(f32[1,128,128]{2,1,0:T(8,128)S(1)} %fusion), channel_id=1, source_target_pairs={{0,4},{4,0},{8,12},{12,8},{1,5},{5,1},{9,13},{13,9},{2,6},{6,2},{1... | collective-permute-start | bytes 196616 | tf_op jit(solution)/shard_map/ppermute | solution.py:41
  116.4 4.3 %collective-permute-start.1 = (f32[1,128,128]{2,1,0:T(8,128)S(1)}, f32[1,128,128]{2,1,0:T(8,128)S(1)}, u32[]{:S(2)}, u32[]{:S(2)}) collective-permute-start(f32[1,128,128]{2,1,0:T(8,128)S(1)} %add.13), channel_id=1, source_target_pairs={{0,8},{4,12},{8,0},{12,4},{1,9},{5,13},{9,1},{13,5},{2,10},{6,14},... | collective-permute-start | bytes 196616 | tf_op jit(solution)/shard_map/ppermute | solution.py:41
  117.9 2.8 %copy-start.3 = (f32[128,128]{1,0:T(8,128)S(1)}, f32[128,128]{1,0:T(8,128)}, u32[]{:S(2)}) copy-start(f32[128,128]{1,0:T(8,128)} %param.7) | copy-start | bytes 196612
Sparse Core Ops, SparseCore 0:
  10.1 32.8 all-gather.1
  45.6 34.2 all-reduce.1
  85.7 27.5 reduce-scatter.1
